TPU v7x, 32 devices: a whole 2x2x4 slice. The times are simulated.
32 devices in a mesh: level: 8 (over z, y), bal: 4 (over x, core).
Axes of the slice: x: 2, y: 2, z: 4, core: 2. Of those that a mesh axis runs over, the one named last changes fastest.
Arguments:
- patches: float32 [640, 5, 4096], P(('level', 'bal')), may hold values from -6 to 6
- patch_ids: int32 [640], P(('level', 'bal')), may hold values from 0 to 639, each once
- live: int32 [32], P(('level', 'bal')), may hold values from 4 to 12, as said below
- counts: int32 [2, 32], P(None, ('level', 'bal')), may hold values from 0 to 4, as said below
- parent_of: int32 [640], replicated, may hold values from 0 to 15
Outputs:
- new_patches: float32 [640, 5, 4096], P(('level', 'bal'))
- new_ids: int32 [640], P(('level', 'bal'))
- coarse: float32 [16, 5, 512], P('level')
Inputs may be any that keep to these rules, and one draw needn't show every extreme that they name: In every level group one device holds exactly 12 live patches. counts[r, d] never exceeds the live patches of device d at the start of round r; in every round and level group some device sends exactly 4.
All inputs are finite; a program needn't handle non-finite values.
Results may differ from a plain program's by a relative error of at most 0.0003.
Values sent between devices are 32-bit elements; how exact they have to be, the bound alone decides.
A program may use at most 64 MiB of HBM per device.

v0:
```python
import jax
import jax.numpy as jnp
from jax import lax
from jax.sharding import PartitionSpec as P

EDGE = 16
VARS = 5
SEND_MOST = 4
PAR_DEV = 2


def from_partner(array, axis, stride):
    return lax.ppermute(array, axis, [(i, i ^ 1 << stride) for i in range(lax.axis_size(axis))])


def restrict(fine_rows):
    leading = fine_rows.shape[:-1]
    half_edge = EDGE // 2
    blocks = fine_rows.reshape(leading + (half_edge, 2, half_edge, 2, half_edge, 2))
    return jnp.mean(blocks, axis=(-5, -3, -1)).reshape(
        leading + (half_edge * half_edge * half_edge,)
    )


def take_top(fine_rows, fine_ids, held_count, sent_count):
    capacity = fine_rows.shape[0]
    lane_index = jnp.arange(SEND_MOST, dtype=jnp.int32)
    pick_index = jnp.clip(held_count - sent_count + lane_index, 0, capacity - 1)
    is_valid = lane_index < sent_count
    return (
        jnp.where(is_valid[:, None, None], fine_rows[pick_index], 0.0),
        jnp.where(is_valid, fine_ids[pick_index], -1),
    )


def place_rows(fine_rows, fine_ids, kept_count, in_rows, in_ids):
    capacity = fine_rows.shape[0]
    slot_index = jnp.arange(capacity, dtype=jnp.int32)
    offset = slot_index - kept_count
    is_hit = (offset >= 0) & (offset < SEND_MOST)
    place_index = jnp.clip(offset, 0, SEND_MOST - 1)
    is_kept = slot_index < kept_count
    new_rows = jnp.where(
        is_kept[:, None, None],
        fine_rows,
        jnp.where(is_hit[:, None, None], in_rows[place_index], 0.0),
    )
    new_ids = jnp.where(is_kept, fine_ids, jnp.where(is_hit, in_ids[place_index], -1))
    return (new_rows, new_ids)


def pairwise_move(fine_rows, fine_ids, held_count, counts, rounds):
    for turn_index in range(rounds):
        sent_count = counts[turn_index, 0]
        out_rows, out_ids = take_top(fine_rows, fine_ids, held_count, sent_count)
        in_rows, in_marks = from_partner((out_rows, out_ids.astype(jnp.float32)), "bal", turn_index)
        in_ids = in_marks.astype(jnp.int32)
        kept_count = held_count - sent_count
        fine_rows, fine_ids = place_rows(fine_rows, fine_ids, kept_count, in_rows, in_ids)
        held_count = kept_count + jnp.sum((in_ids >= 0).astype(jnp.int32))
    return (fine_rows, fine_ids)


def parent_sums(fine_rows, fine_ids, parent_of):
    capacity = fine_rows.shape[0]
    reduced = restrict(fine_rows).reshape(capacity, -1)
    parent = jnp.where(fine_ids >= 0, parent_of[jnp.clip(fine_ids, 0, parent_of.shape[0] - 1)], -1)
    wanted = jnp.arange(lax.axis_size("level") * PAR_DEV, dtype=jnp.int32)
    one_hot = (wanted[:, None] == parent[None, :]).astype(jnp.float32)
    level_sums = lax.psum_scatter(
        jnp.dot(one_hot, reduced, precision=lax.Precision.HIGHEST),
        "level",
        scatter_dimension=0,
        tiled=True,
    )
    group_sums = lax.psum(level_sums, "bal")
    return group_sums.reshape(PAR_DEV, VARS, -1)


def per_device(patches, patch_ids, live, counts, parent_of):
    capacity = patches.shape[0]
    group = lax.axis_size("bal")
    rounds = group.bit_length() - 1
    slot_index = jnp.arange(capacity, dtype=jnp.int32)
    held_count = live[0]
    is_kept = slot_index < held_count
    fine_rows = jnp.where(is_kept[:, None, None], patches, 0.0)
    fine_ids = jnp.where(is_kept, patch_ids, -1)
    coarse = parent_sums(fine_rows, fine_ids, parent_of)
    fine_rows, fine_ids = pairwise_move(fine_rows, fine_ids, held_count, counts, rounds)
    return (fine_rows, fine_ids, coarse)


def solution(mesh):
    return jax.shard_map(
        per_device,
        mesh=mesh,
        in_specs=(
            P(("level", "bal"), None, None),
            P(("level", "bal")),
            P(("level", "bal")),
            P(None, ("level", "bal")),
            P(),
        ),
        out_specs=(P(("level", "bal"), None, None), P(("level", "bal")), P("level", None, None)),
        check_vma=False,
    )
```

profile of v0, /device:TPU:0, one launch (start us, length us, event | category | flops | bytes accessed | tf_op | source)
XLA Modules:
  0.0 143.0 jit_solution(11142344460428278387)
XLA Ops:
  7.2 1.3 fusion.13
  10.4 2.7 %copy_select_fusion = f32[20,5,4096]{2,1,0:T(8,128)S(1)} fusion(f32[20,5,4096]{2,0,1:T(8,128)} %param.5, pred[20]{0:T(512)(128)(4,1)S(1)} %iota_compare_fusion.4), kind=kLoop, calls=%fused_computation.7 | loop fusion | flops 409600 | bytes 3276820 | tf_op jit(solution)/shard_map/jit(_where)/select_n | solution.py:87
  13.7 0.9 broadcast_select_fusion.1
  16.4 6.2 %copy.14 = f32[20,5,4096]{0,2,1:T(8,128)} copy(f32[20,5,4096]{2,1,0:T(8,128)S(1)} %copy_select_fusion) | data formatting | bytes 3276800 | tf_op jit(solution)/shard_map/jit(_where)/select_n | solution.py:87
  22.6 0.6 iota_compare_fusion.2
  23.3 10.6 %reduce_sum.19 = f32[20,5,8,8,8]{0,4,3,2,1:T(8,128)S(1)} reduce(f32[20,5,8,2,8,2,8,2]{0,7,6,5,4,3,2,1:T(2,128)} %bitcast.30, f32[]{:T(128)} %constant.3.clone.1), dimensions={3,5,7}, to_apply=%region_1.2 | reduce | flops 358400 | bytes 1843204 | tf_op jit(solution)/shard_map/reduce_sum | solution.py:20
  34.1 0.7 gather_fusion.6
  38.0 0.7 fusion.12
  38.7 2.5 %compare_select_fusion.11 = (s32[20]{0:T(128)S(1)}, s32[20]{0:T(128)S(1)}) fusion(s32[20]{0:T(128)S(1)} %gather_fusion.6, s32[20]{0:T(128)S(1)} %get-tuple-element.10, s32[]{:T(128)} %bitcast.10, s32[]{:T(128)} %bitcast.9, s32[]{:T(128)} %bitcast.8, s32[]{:T(128)} %bitcast.7, s32[]{:T(128)S(6)} %sub.42), kind=kLoop, calls=%fused_computation.32 | loop fusion | flops 400 | bytes 340 | tf_op jit(solution)/shard_map/jit(_where)/select_n | solution.py:67
  41.8 0.7 select_convert_fusion
  42.5 3.0 %collective-permute-start.3 = (f32[4]{0:T(128)S(1)}, f32[4]{0:T(128)S(1)}, u32[]{:S(2)}, u32[]{:S(2)}) collective-permute-start(f32[4]{0:T(128)S(1)} %select_convert_fusion), channel_id=1, source_target_pairs={{0,2},{1,3},{2,0},{3,1},{4,6},{5,7},{6,4},{7,5},{8,10},{9,11},{10,... | collective-permute-start | bytes 56 | tf_op jit(solution)/shard_map/ppermute | solution.py:13
  45.5 1.4 fusion
  47.0 0.7 fusion.11
  47.7 3.0 %fusion.5 = s32[20]{0:T(128)} fusion(s32[20]{0:T(128)S(1)} %get-tuple-element.12, s32[]{:T(128)} %bitcast.11, s32[]{:T(128)} %bitcast.12, s32[]{:T(128)} %bitcast.13, s32[]{:T(128)} %bitcast.14, s32[]{:T(128)S(6)} %sub.43), kind=kLoop, calls=%fused_computation.39 | loop fusion | flops 360 | bytes 180 | tf_op jit(solution)/shard_map/jit(_where)/select_n | solution.py:48
  50.7 2.2 %gather_fusion.2 = f32[20,5,4096]{2,1,0:T(8,128)} fusion(f32[4,5,4096]{2,1,0:T(8,128)S(1)} %collective-permute-done.1, s32[1024]{0:T(1024)S(1)} %pad_clamp_fusion.3), kind=kCustom, calls=%fused_computation.2 | custom fusion | bytes 3276880 | tf_op jit(solution)/shard_map/gather | solution.py:46
  52.9 3.8 %select_select_fusion.1 = f32[20,5,4096]{2,1,0:T(8,128)S(1)} fusion(f32[20,5,4096]{2,1,0:T(8,128)} %gather_fusion.2, pred[20]{0:T(512)(128)(4,1)S(1)} %get-tuple-element.23, pred[20]{0:T(512)(128)(4,1)S(1)} %get-tuple-element.24, f32[20,5,4096]{2,0,1:T(8,128)} %param.5, pred[20]{0:T(512)(128)(4,1)S(1)} %iota_compare_fusion.4), kind=kLoop, calls=%fused_computation.9 | loop fusion | flops 1228800 | bytes 4915260 | tf_op jit(solution)/shard_map/jit(_where)/select_n | solution.py:43
  57.3 0.9 broadcast_select_fusion
  58.2 2.0 %collective-permute-start.2 = (f32[4,5,4096]{2,1,0:T(8,128)}, f32[4,5,4096]{2,1,0:T(8,128)S(1)}, u32[]{:S(2)}, u32[]{:S(2)}) collective-permute-start(f32[4,5,4096]{2,1,0:T(8,128)} %broadcast_select_fusion), channel_id=1, source_target_pairs={{0,2},{1,3},{2,0},{3,1},{4,6},{5,7},{6,4},{7,5},{8,10},{9,11},{10,... | collective-permute-start | bytes 983048 | tf_op jit(solution)/shard_map/ppermute | solution.py:13
  60.3 57.1 %all-reduce.3.cloned.1.call-done = f32[16,2560]{1,0:T(8,128)} async-done(((f32[16,2560]{1,0:T(8,128)}), f32[16,2560]{1,0:T(8,128)}) %all-reduce.3.cloned.1.call-update) | async-done | bytes 163856
  117.4 0.9 constant_dynamic-slice_fusion
  118.3 10.3 %psum.7 = f32[2,5,512]{2,1,0:T(8,128)S(1)} all-reduce(f32[2,5,512]{2,1,0:T(8,128)S(1)} %reshape.127), channel_id=1, replica_groups=mesh['level'=8,'bal'=4] {'bal'}, use_global_device_ids=true, to_apply=%region_3.4 | all-reduce | flops 5120 | bytes 40960 | tf_op jit(solution)/shard_map/psum | solution.py:76
  129.2 2.2 %gather_fusion.4 = f32[20,5,4096]{2,1,0:T(8,128)} fusion(f32[4,5,4096]{2,1,0:T(8,128)S(1)} %collective-permute-done.2, s32[1024]{0:T(1024)S(1)} %pad_clamp_fusion.1), kind=kCustom, calls=%fused_computation.4 | custom fusion | bytes 3276880 | tf_op jit(solution)/shard_map/gather | solution.py:46
  131.5 2.4 %select_select_fusion = f32[20,5,4096]{2,1,0:T(8,128)S(1)} fusion(f32[20,5,4096]{2,1,0:T(8,128)S(1)} %select_select_fusion.1, f32[20,5,4096]{2,1,0:T(8,128)} %gather_fusion.4, pred[20]{0:T(512)(128)(4,1)S(1)} %get-tuple-element.25, pred[20]{0:T(512)(128)(4,1)S(1)} %get-tuple-element.26), kind=kLoop, calls=%fused_computation.8 | loop fusion | flops 819200 | bytes 4915240 | tf_op jit(solution)/shard_map/jit(_where)/select_n | solution.py:43
  133.9 2.2 %copy.15 = f32[20,5,4096]{2,0,1:T(8,128)} copy(f32[20,5,4096]{2,1,0:T(8,128)S(1)} %select_select_fusion) | data formatting | bytes 3276800
  (40 shorter events, 6.5 us)
Async XLA Ops:
  7.2 26.9 %copy-start = (s32[640]{0:T(1024)S(1)}, s32[640]{0:T(1024)}, u32[]{:S(2)}) copy-start(s32[640]{0:T(1024)} %param.9) | copy-start | bytes 7684
  7.2 110.2 %all-reduce.3.cloned.1.call-start = ((), (), s32[]{:S(2)}) async-start(), calls=%async_computation | async-start | bytes 327680
  10.4 4.7 %copy-start.1 = (s32[20]{0:T(128)S(1)}, s32[20]{0:T(128)}, u32[]{:S(2)}) copy-start(s32[20]{0:T(128)} %param.6) | copy-start | bytes 244
  14.6 36.1 %collective-permute-start.1 = (f32[4,5,4096]{2,1,0:T(8,128)}, f32[4,5,4096]{2,1,0:T(8,128)S(1)}, u32[]{:S(2)}, u32[]{:S(2)}) collective-permute-start(f32[4,5,4096]{2,1,0:T(8,128)} %broadcast_select_fusion.1), channel_id=1, source_target_pairs={{0,1},{1,0},{2,3},{3,2},{4,5},{5,4},{6,7},{7,6},{8,9},{9,8},{10,11... | collective-permute-start | bytes 983048 | tf_op jit(solution)/shard_map/ppermute | solution.py:13
  16.3 19.7 %collective-permute-start = (f32[4]{0:T(128)S(1)}, f32[4]{0:T(128)S(1)}, u32[]{:S(2)}, u32[]{:S(2)}) collective-permute-start(f32[4]{0:T(128)S(1)} %select_convert_fusion.1), channel_id=1, source_target_pairs={{0,1},{1,0},{2,3},{3,2},{4,5},{5,4},{6,7},{7,6},{8,9},{9,8},{10,11... | collective-permute-start | bytes 56 | tf_op jit(solution)/shard_map/ppermute | solution.py:13
  33.9 0.9 copy-start.2
  42.5 4.6 %collective-permute-start.3 = (f32[4]{0:T(128)S(1)}, f32[4]{0:T(128)S(1)}, u32[]{:S(2)}, u32[]{:S(2)}) collective-permute-start(f32[4]{0:T(128)S(1)} %select_convert_fusion), channel_id=1, source_target_pairs={{0,2},{1,3},{2,0},{3,1},{4,6},{5,7},{6,4},{7,5},{8,10},{9,11},{10,... | collective-permute-start | bytes 56 | tf_op jit(solution)/shard_map/ppermute | solution.py:13
  58.2 71.0 %collective-permute-start.2 = (f32[4,5,4096]{2,1,0:T(8,128)}, f32[4,5,4096]{2,1,0:T(8,128)S(1)}, u32[]{:S(2)}, u32[]{:S(2)}) collective-permute-start(f32[4,5,4096]{2,1,0:T(8,128)} %broadcast_select_fusion), channel_id=1, source_target_pairs={{0,2},{1,3},{2,0},{3,1},{4,6},{5,7},{6,4},{7,5},{8,10},{9,11},{10,... | collective-permute-start | bytes 983048 | tf_op jit(solution)/shard_map/ppermute | solution.py:13
Sparse Core Ops, SparseCore 0:
  47.0 70.3 all-reduce.2
where the time goes:
time: 144 us; the launch traced here: 143 us
  waiting for transfers between devices  57.3 us (40%)
  other arithmetic  30.1 us (21%)
  local copies, waits for them, and re-layouts  20.8 us (14%)
  between operations  17.4 us (12%)
  blocking collectives  10.3 us (7%)
  starting transfers between devices  5.65 us (4%)
    unnamed x2, waiting for transfers between devices  57.2 us
    reduce_sum x1, other arithmetic, restrict(): jnp.mean(blocks, axis=(-5, -3, -1))  10.6 us
    psum x1, blocking collectives, parent_sums(): group_sums = lax.psum(level_sums, 'bal')  10.3 us
    select_n x2, other arithmetic, place_rows(): jnp.where(is_kept[:, None, None], fine_rows, jnp.where(is_hit[:, None, No...  6.28 us
    select_n x1, local copies, waits for them, and re-layouts, per_device(): fine_rows = jnp.where(is_kept[:, None, None], patches, 0.0)  6.24 us
    ppermute x4, starting transfers between devices, from_partner(): lax.ppermute(array, axis, [(i, i ^ 1 << stride) for i in range(lax.axis_s...  5.62 us
    gather x2, local copies, waits for them, and re-layouts, place_rows(): in_rows[place_index]  4.45 us
    unnamed x10, local copies, waits for them, and re-layouts  4.34 us
  transfers between devices with their start and end apart: 5, of which 2 were waited for; matrix products, arithmetic and copies ran while one was open for 28% of the time, Pallas kernels for 0%

commit v1 on v0

--- a/solution.py
+++ b/solution.py
@@ -73,7 +73,11 @@
         scatter_dimension=0,
         tiled=True,
     )
-    group_sums = lax.psum(level_sums, "bal")
+    group_sums = level_sums
+    for hop in (1, 2):
+        group_sums = group_sums + lax.ppermute(
+            group_sums, "bal", [(dev, dev ^ hop) for dev in range(4)]
+        )
     return group_sums.reshape(PAR_DEV, VARS, -1)
 
 

time: 144 us -> 154 us (1.069)
  waiting for transfers between devices: 57.3 us -> 76.8 us
  blocking collectives: 10.3 us -> 0 us
    psum x1 -> x0, blocking collectives: 10.3 us -> none  [parent_sums(): group_sums = lax.psum(level_sums, 'bal')]
    unnamed x2, waiting for transfers between devices: 57.2 us -> 66.4 us
    ppermute x0 -> x2, waiting for transfers between devices: none -> 8.85 us  [parent_sums(): lax.ppermute(group_sums, 'bal', [(dev, dev ^ hop) for dev in range(4)])]
    unnamed x10 -> x7, local copies, waits for them, and re-layouts: 4.34 us -> 3.71 us
  transfers between devices with their start and end apart: 5 -> 7, of which waited for: 2 -> 3; matrix products, arithmetic and copies ran while one was open for 28% -> 28% of each run, Pallas kernels for 0% -> 0%
where the time goes in v1:
time: 154 us; the launch traced here: 153 us
  waiting for transfers between devices  76.8 us (50%)
  other arithmetic  31.5 us (20%)
  local copies, waits for them, and re-layouts  20.1 us (13%)
  between operations  17.5 us (11%)
  starting transfers between devices  5.87 us (4%)
    unnamed x2, waiting for transfers between devices  66.4 us
    reduce_sum x1, other arithmetic, restrict(): jnp.mean(blocks, axis=(-5, -3, -1))  10.6 us
    ppermute x2, waiting for transfers between devices, parent_sums(): lax.ppermute(group_sums, 'bal', [(dev, dev ^ hop) for dev in range(4)])  8.85 us
    select_n x1, local copies, waits for them, and re-layouts, per_device(): fine_rows = jnp.where(is_kept[:, None, None], patches, 0.0)  6.25 us
    select_n x2, other arithmetic, place_rows(): jnp.where(is_kept[:, None, None], fine_rows, jnp.where(is_hit[:, None, No...  6.12 us
    ppermute x4, starting transfers between devices, from_partner(): lax.ppermute(array, axis, [(i, i ^ 1 << stride) for i in range(lax.axis_s...  5.17 us
    gather x2, local copies, waits for them, and re-layouts, place_rows(): in_rows[place_index]  4.45 us
    unnamed x7, local copies, waits for them, and re-layouts  3.71 us
  transfers between devices with their start and end apart: 7, of which 3 were waited for; matrix products, arithmetic and copies ran while one was open for 28% of the time, Pallas kernels for 0%

profile of v1, /device:TPU:0, one launch (start us, length us, event | category | flops | bytes accessed | tf_op | source)
XLA Modules:
  0.0 153.2 jit_solution(4822100619434258024)
XLA Ops:
  7.2 1.3 fusion.13
  9.9 0.7 compare_select_fusion
  13.1 2.7 %copy_select_fusion = f32[20,5,4096]{2,1,0:T(8,128)S(1)} fusion(f32[20,5,4096]{2,0,1:T(8,128)} %param.5, pred[20]{0:T(512)(128)(4,1)S(1)} %iota_compare_fusion.4), kind=kLoop, calls=%fused_computation.7 | loop fusion | flops 409600 | bytes 3276820 | tf_op jit(solution)/shard_map/jit(_where)/select_n | solution.py:91
  16.3 0.9 broadcast_select_fusion.1
  17.3 6.2 %copy.14 = f32[20,5,4096]{0,2,1:T(8,128)} copy(f32[20,5,4096]{2,1,0:T(8,128)S(1)} %copy_select_fusion) | data formatting | bytes 3276800 | tf_op jit(solution)/shard_map/jit(_where)/select_n | solution.py:91
  23.6 10.6 %reduce_sum.19 = f32[20,5,8,8,8]{0,4,3,2,1:T(8,128)S(1)} reduce(f32[20,5,8,2,8,2,8,2]{0,7,6,5,4,3,2,1:T(2,128)} %bitcast.31, f32[]{:T(128)} %constant.3.clone.1), dimensions={3,5,7}, to_apply=%region_1.2 | reduce | flops 358400 | bytes 1843204 | tf_op jit(solution)/shard_map/reduce_sum | solution.py:20
  34.3 0.7 iota_compare_fusion.2
  35.0 0.7 gather_fusion.6
  38.9 0.7 fusion.12
  39.5 2.5 %compare_select_fusion.11 = (s32[20]{0:T(128)S(1)}, s32[20]{0:T(128)S(1)}) fusion(s32[20]{0:T(128)S(1)} %gather_fusion.6, s32[20]{0:T(128)S(1)} %get-tuple-element.13, s32[]{:T(128)} %bitcast.10, s32[]{:T(128)} %bitcast.9, s32[]{:T(128)} %bitcast.8, s32[]{:T(128)} %bitcast.7, s32[]{:T(128)S(6)} %sub.42), kind=kLoop, calls=%fused_computation.32 | loop fusion | flops 400 | bytes 340 | tf_op jit(solution)/shard_map/jit(_where)/select_n | solution.py:67
  42.1 1.4 fusion
  44.8 3.0 %collective-permute-start.3 = (f32[4]{0:T(128)S(1)}, f32[4]{0:T(128)S(1)}, u32[]{:S(2)}, u32[]{:S(2)}) collective-permute-start(f32[4]{0:T(128)S(1)} %select_convert_fusion), channel_id=1, source_target_pairs={{0,2},{1,3},{2,0},{3,1},{4,6},{5,7},{6,4},{7,5},{8,10},{9,11},{10,... | collective-permute-start | bytes 56 | tf_op jit(solution)/shard_map/ppermute | solution.py:13
  47.9 1.5 %collective-permute-done.3 = f32[4]{0:T(128)S(1)} collective-permute-done((f32[4]{0:T(128)S(1)}, f32[4]{0:T(128)S(1)}, u32[]{:S(2)}, u32[]{:S(2)}) %collective-permute-start.3) | collective-permute-done | bytes 48 | tf_op jit(solution)/shard_map/ppermute | solution.py:13
  50.0 66.3 %all-reduce.3.cloned.1.call-done = f32[16,2560]{1,0:T(8,128)} async-done(((f32[16,2560]{1,0:T(8,128)}), f32[16,2560]{1,0:T(8,128)}) %all-reduce.3.cloned.1.call-update) | async-done | bytes 163856
  116.4 0.9 constant_dynamic-slice_fusion
  117.4 2.2 %gather_fusion.2 = f32[20,5,4096]{2,1,0:T(8,128)} fusion(f32[4,5,4096]{2,1,0:T(8,128)S(1)} %collective-permute-done.1, s32[1024]{0:T(1024)S(1)} %pad_clamp_fusion.3), kind=kCustom, calls=%fused_computation.2 | custom fusion | bytes 3276880 | tf_op jit(solution)/shard_map/gather | solution.py:46
  119.6 3.8 %select_select_fusion.1 = f32[20,5,4096]{2,1,0:T(8,128)S(1)} fusion(f32[20,5,4096]{2,1,0:T(8,128)} %gather_fusion.2, pred[20]{0:T(512)(128)(4,1)S(1)} %get-tuple-element.26, pred[20]{0:T(512)(128)(4,1)S(1)} %get-tuple-element.27, f32[20,5,4096]{2,0,1:T(8,128)} %param.5, pred[20]{0:T(512)(128)(4,1)S(1)} %iota_compare_fusion.4), kind=kLoop, calls=%fused_computation.9 | loop fusion | flops 1228800 | bytes 4915260 | tf_op jit(solution)/shard_map/jit(_where)/select_n | solution.py:43
  124.2 1.6 %collective-permute-start.2 = (f32[4,5,4096]{2,1,0:T(8,128)S(1)}, f32[4,5,4096]{2,1,0:T(8,128)S(1)}, u32[]{:S(2)}, u32[]{:S(2)}) collective-permute-start(f32[4,5,4096]{2,1,0:T(8,128)S(1)} %broadcast_select_fusion), channel_id=1, source_target_pairs={{0,2},{1,3},{2,0},{3,1},{4,6},{5,7},{6,4},{7,5},{8,10},{9,11},{10,... | collective-permute-start | bytes 983048 | tf_op jit(solution)/shard_map/ppermute | solution.py:13
  125.7 0.9 fusion.15
  127.2 2.9 %fusion.5 = s32[20]{0:T(128)} fusion(s32[20]{0:T(128)S(1)} %get-tuple-element.15, s32[]{:T(128)} %bitcast.11, s32[]{:T(128)} %bitcast.12, s32[]{:T(128)} %bitcast.13, s32[]{:T(128)} %bitcast.14, s32[]{:T(128)S(6)} %sub.43), kind=kLoop, calls=%fused_computation.39 | loop fusion | flops 360 | bytes 180 | tf_op jit(solution)/shard_map/jit(_where)/select_n | solution.py:48
  130.1 8.8 %collective-permute-done.5 = f32[2,2560]{1,0:T(2,128)S(1)} collective-permute-done((f32[2,2560]{1,0:T(2,128)S(1)}, f32[2,2560]{1,0:T(2,128)S(1)}, u32[]{:S(2)}, u32[]{:S(2)}) %collective-permute-start.5) | collective-permute-done | bytes 20512 | tf_op jit(solution)/shard_map/ppermute | solution.py:78
  139.6 2.2 %gather_fusion.4 = f32[20,5,4096]{2,1,0:T(8,128)} fusion(f32[4,5,4096]{2,1,0:T(8,128)S(1)} %collective-permute-done.2, s32[1024]{0:T(1024)S(1)} %pad_clamp_fusion.1), kind=kCustom, calls=%fused_computation.4 | custom fusion | bytes 3276880 | tf_op jit(solution)/shard_map/gather | solution.py:46
  141.8 2.3 %select_select_fusion = f32[20,5,4096]{2,1,0:T(8,128)S(1)} fusion(f32[20,5,4096]{2,1,0:T(8,128)S(1)} %select_select_fusion.1, f32[20,5,4096]{2,1,0:T(8,128)} %gather_fusion.4, pred[20]{0:T(512)(128)(4,1)S(1)} %get-tuple-element.28, pred[20]{0:T(512)(128)(4,1)S(1)} %get-tuple-element.29), kind=kLoop, calls=%fused_computation.8 | loop fusion | flops 819200 | bytes 4915240 | tf_op jit(solution)/shard_map/jit(_where)/select_n | solution.py:43
  144.1 2.2 %copy.15 = f32[20,5,4096]{2,0,1:T(8,128)} copy(f32[20,5,4096]{2,1,0:T(8,128)S(1)} %select_select_fusion) | data formatting | bytes 3276800
  (41 shorter events, 8.5 us)
Async XLA Ops:
  7.2 27.8 %copy-start = (s32[640]{0:T(1024)S(1)}, s32[640]{0:T(1024)}, u32[]{:S(2)}) copy-start(s32[640]{0:T(1024)} %param.9) | copy-start | bytes 7684
  7.2 109.2 %all-reduce.3.cloned.1.call-start = ((), (), s32[]{:S(2)}) async-start(), calls=%async_computation | async-start | bytes 327680
  11.8 25.1 %collective-permute-start = (f32[4]{0:T(128)S(1)}, f32[4]{0:T(128)S(1)}, u32[]{:S(2)}, u32[]{:S(2)}) collective-permute-start(f32[4]{0:T(128)S(1)} %select_convert_fusion.1), channel_id=1, source_target_pairs={{0,1},{1,0},{2,3},{3,2},{4,5},{5,4},{6,7},{7,6},{8,9},{9,8},{10,11... | collective-permute-start | bytes 56 | tf_op jit(solution)/shard_map/ppermute | solution.py:13
  17.3 100.1 %collective-permute-start.1 = (f32[4,5,4096]{2,1,0:T(8,128)}, f32[4,5,4096]{2,1,0:T(8,128)S(1)}, u32[]{:S(2)}, u32[]{:S(2)}) collective-permute-start(f32[4,5,4096]{2,1,0:T(8,128)} %broadcast_select_fusion.1), channel_id=1, source_target_pairs={{0,1},{1,0},{2,3},{3,2},{4,5},{5,4},{6,7},{7,6},{8,9},{9,8},{10,11... | collective-permute-start | bytes 983048 | tf_op jit(solution)/shard_map/ppermute | solution.py:13
  34.1 1.5 copy-start.1
  44.8 4.6 %collective-permute-start.3 = (f32[4]{0:T(128)S(1)}, f32[4]{0:T(128)S(1)}, u32[]{:S(2)}, u32[]{:S(2)}) collective-permute-start(f32[4]{0:T(128)S(1)} %select_convert_fusion), channel_id=1, source_target_pairs={{0,2},{1,3},{2,0},{3,1},{4,6},{5,7},{6,4},{7,5},{8,10},{9,11},{10,... | collective-permute-start | bytes 56 | tf_op jit(solution)/shard_map/ppermute | solution.py:13
  117.3 8.4 %collective-permute-start.4 = (f32[2,2560]{1,0:T(2,128)S(1)}, f32[2,2560]{1,0:T(2,128)S(1)}, u32[]{:S(2)}, u32[]{:S(2)}) collective-permute-start(f32[2,2560]{1,0:T(2,128)S(1)} %constant_dynamic-slice_fusion), channel_id=1, source_target_pairs={{0,1},{1,0},{2,3},{3,2},{4,5},{5,4},{6,7},{7,6},{8,9},{9,8},{10,11... | collective-permute-start | bytes 61448 | tf_op jit(solution)/shard_map/ppermute | solution.py:78
  124.2 15.4 %collective-permute-start.2 = (f32[4,5,4096]{2,1,0:T(8,128)S(1)}, f32[4,5,4096]{2,1,0:T(8,128)S(1)}, u32[]{:S(2)}, u32[]{:S(2)}) collective-permute-start(f32[4,5,4096]{2,1,0:T(8,128)S(1)} %broadcast_select_fusion), channel_id=1, source_target_pairs={{0,2},{1,3},{2,0},{3,1},{4,6},{5,7},{6,4},{7,5},{8,10},{9,11},{10,... | collective-permute-start | bytes 983048 | tf_op jit(solution)/shard_map/ppermute | solution.py:13
  126.6 12.3 %collective-permute-start.5 = (f32[2,2560]{1,0:T(2,128)S(1)}, f32[2,2560]{1,0:T(2,128)S(1)}, u32[]{:S(2)}, u32[]{:S(2)}) collective-permute-start(f32[2,2560]{1,0:T(2,128)S(1)} %fusion.15), channel_id=1, source_target_pairs={{0,2},{1,3},{2,0},{3,1},{4,6},{5,7},{6,4},{7,5},{8,10},{9,11},{10,... | collective-permute-start | bytes 61448 | tf_op jit(solution)/shard_map/ppermute | solution.py:78
Sparse Core Ops, SparseCore 0:
  43.6 72.7 all-reduce.2
